TPU v7x, 128 devices: a whole 4x4x4 slice. The times are simulated.
128 devices in a mesh: row: 8 (over z, core), col: 16 (over x, y).
Axes of the slice: x: 4, y: 4, z: 4, core: 2. Of those that a mesh axis runs over, the one named last changes fastest.
Arguments:
- normed: bfloat16 [8192, 7168], P(None, 'col'), may hold values from -44 to 44
- projection_weight: bfloat16 [7168, 3, 7168], P('col', None, 'row')
- adapter_down_weight: bfloat16 [7168, 16, 32], P(None, 'col'), may hold values from -0.0625 to 0.0625
- adapter_up_weight: bfloat16 [16, 2, 16, 7168], P(None, None, None, 'row'), may hold values from -0.47851562 to 0.47851562
- packed_prompt_length: int32 [64], replicated, may hold values from 64 to 512, as said below
- prompt_adapter_ids: int32 [64], replicated, may hold values from 0 to 63, as said below
- slot_adapter_ids: int32 [16], replicated, may hold values from 0 to 63, as said below
- prompt_page_slots: int32 [64, 4], replicated, may hold values from -1 to 159, as said below
Outputs:
- attended: bfloat16 [8192, 7168], P('col', 'row')
- kv_cache: bfloat16 [160, 128, 2, 7168], P('col', None, None, 'row')
Inputs may be any that keep to these rules, and one draw needn't show every extreme that they name: `packed_prompt_length`: the 64 lengths sum to 8192; one of them is exactly 512 and one exactly 64. `slot_adapter_ids`: distinct adapter ids. `prompt_adapter_ids`: every entry is one of slot_adapter_ids, and every loaded adapter is named by at least one prompt. `prompt_page_slots`: entry [i, j] is -1 where 128 * j >= packed_prompt_length[i]; otherwise it lies among slots 10 * c to 10 * c + 9, where c is the block of 512 packed tokens that holds the page's last token. No slot is named twice.
All inputs are finite; a program needn't handle non-finite values.
Results may differ from a plain program's by a relative error of at most 0.0072.
Values may be sent and summed in bfloat16 or wider, within the bound.
A program may use at most 256 MiB of HBM per device.

v0:
```python
import jax
import jax.numpy as jnp
from jax import lax
from jax.sharding import PartitionSpec as P

HEAD_DIM = 128
PAGE = 128
NEAR = 1
SLOTS_DEV = 10
adapter_scale = 2.0
masked_score = -1e30


def shifted(block, axis, distance):
    devices = range(lax.axis_size(axis))
    route = [(i - distance, i) for i in devices if i - distance in devices]
    return lax.ppermute(block, axis, route)


def start_table(packed_prompt_length):
    prompt_ends = jnp.cumsum(packed_prompt_length)
    return prompt_ends - packed_prompt_length


def slot_table(prompt_adapter_ids, slot_adapter_ids):
    active_slots = slot_adapter_ids.shape[0]
    matched = slot_adapter_ids[None, :] == prompt_adapter_ids[:, None]
    return jnp.sum(
        jnp.where(matched, jnp.arange(active_slots, dtype=jnp.int32)[None, :], 0), axis=1
    )


def token_prompts(positions, prompt_starts):
    inside = (positions[:, None] >= prompt_starts[None, :]).astype(jnp.int32)
    return jnp.sum(inside, axis=1) - 1


def token_slots(prompts, slot_of):
    prompt_count = slot_of.shape[0]
    onehot = prompts[:, None] == jnp.arange(prompt_count, dtype=jnp.int32)[None, :]
    return jnp.sum(jnp.where(onehot, slot_of[None, :], 0), axis=1)


def down_term(row_block, slots_here, down_cols, active_slots):
    combined_output = jnp.dot(row_block, down_cols, preferred_element_type=jnp.float32)
    combined_output = combined_output.reshape(row_block.shape[0], active_slots, -1)
    pick_slot = slots_here[:, None] == jnp.arange(active_slots, dtype=jnp.int32)[None, :]
    return jnp.sum(jnp.where(pick_slot[:, :, None], combined_output, 0.0), axis=1)


def local(
    normed,
    projection_weight,
    adapter_down_weight,
    adapter_up_weight,
    packed_prompt_length,
    prompt_adapter_ids,
    slot_adapter_ids,
    prompt_page_slots,
):
    col_count = lax.axis_size("col")
    row_count = lax.axis_size("row")
    col_index = lax.axis_index("col")
    my_row = lax.axis_index("row")
    tok_all, width_loc = normed.shape
    tok_blk = tok_all // col_count
    head_column_span = projection_weight.shape[2]
    heads_loc = head_column_span // HEAD_DIM
    active_slots = slot_adapter_ids.shape[0]
    adapter_rank_width = adapter_up_weight.shape[2]
    prompt_starts = start_table(packed_prompt_length)
    slot_of = slot_table(prompt_adapter_ids, slot_adapter_ids)
    block_start = col_index * tok_blk
    mine = block_start + jnp.arange(tok_blk, dtype=jnp.int32)
    mine_prompts = token_prompts(mine, prompt_starts)
    mine_slots = token_slots(mine_prompts, slot_of)
    down_weight_slices = lax.all_to_all(
        adapter_down_weight, "col", split_axis=0, concat_axis=1, tiled=True
    )
    down_cols = down_weight_slices.reshape(width_loc, -1)
    own_rows = lax.all_to_all(normed, "col", split_axis=0, concat_axis=1, tiled=True)
    weight_piece = lax.all_gather(projection_weight, "col", axis=0, tiled=True)
    flat_piece = weight_piece.reshape(weight_piece.shape[0], -1)
    projection_total = jnp.dot(own_rows, flat_piece, preferred_element_type=jnp.float32)
    rows_per = tok_all // row_count
    row_first = my_row * rows_per
    row_positions = row_first + jnp.arange(rows_per, dtype=jnp.int32)
    row_slots = token_slots(token_prompts(row_positions, prompt_starts), slot_of)
    row_part = lax.dynamic_slice_in_dim(normed, row_first, rows_per, 0)
    summed = lax.psum(down_term(row_part, row_slots, down_cols, active_slots), "col")
    down_every = lax.all_gather(summed.astype(jnp.bfloat16), "row", axis=0, tiled=True)
    local_down_output = lax.dynamic_slice_in_dim(down_every, block_start, tok_blk, 0)
    pick_half = (mine_slots[:, None] == jnp.arange(active_slots, dtype=jnp.int32)[None, :]).astype(
        jnp.bfloat16
    )

    def reduced_rank_rows(low_part, slot_membership):
        token_spread = (pick_half[:, :, None] * low_part[:, None, :]).reshape(
            tok_blk, active_slots * adapter_rank_width
        )
        up_weight_table = adapter_up_weight[:, slot_membership].reshape(
            active_slots * adapter_rank_width, head_column_span
        )
        return jnp.dot(token_spread, up_weight_table, preferred_element_type=jnp.float32)

    query_token_rows = (
        projection_total[:, :head_column_span]
        + adapter_scale * reduced_rank_rows(local_down_output[:, :adapter_rank_width], 0)
    ).astype(jnp.bfloat16)
    key_rows = projection_total[:, head_column_span : 2 * head_column_span].astype(jnp.bfloat16)
    value_token_rows = (
        projection_total[:, 2 * head_column_span :]
        + adapter_scale * reduced_rank_rows(local_down_output[:, adapter_rank_width:], 1)
    ).astype(jnp.bfloat16)
    own_kv = jnp.stack([key_rows, value_token_rows], axis=1)
    earlier = [shifted(own_kv, "col", 1)]
    window = jnp.concatenate(earlier[::-1] + [own_kv], axis=0)
    window_len = window.shape[0]
    window_pos = block_start - NEAR * tok_blk + jnp.arange(window_len, dtype=jnp.int32)
    window_prompts = token_prompts(window_pos, prompt_starts)
    allowed = (mine_prompts[:, None] == window_prompts[None, :]) & (
        window_pos[None, :] <= mine[:, None]
    )
    query_heads = query_token_rows.reshape(tok_blk, heads_loc, HEAD_DIM)
    key_heads = window[:, 0].reshape(window_len, heads_loc, HEAD_DIM)
    value_heads = window[:, 1].reshape(window_len, heads_loc, HEAD_DIM)
    score_scale = HEAD_DIM ** (-0.5)
    scores = (
        jnp.einsum("qhd,khd->hqk", query_heads, key_heads, preferred_element_type=jnp.float32)
        * score_scale
    )
    limited = jnp.where(allowed[None], scores, masked_score)
    peak_score = jnp.max(limited, axis=2, keepdims=True)
    weight = jnp.where(allowed[None], jnp.exp(scores - peak_score), 0.0)
    denominator = jnp.sum(weight, axis=2)
    mixed_heads = jnp.einsum(
        "hqk,khd->qhd", weight.astype(jnp.bfloat16), value_heads, preferred_element_type=jnp.float32
    )
    attended = (
        (mixed_heads / jnp.transpose(denominator)[:, :, None])
        .reshape(tok_blk, head_column_span)
        .astype(jnp.bfloat16)
    )
    prev_kv = earlier[0]
    page_window = jnp.concatenate(
        [prev_kv, own_kv, jnp.zeros((PAGE, 2, head_column_span), jnp.bfloat16)], axis=0
    )
    max_pages = prompt_page_slots.shape[1]
    lens_rep = jnp.repeat(packed_prompt_length, max_pages)
    starts_rep = jnp.repeat(prompt_starts, max_pages)
    page_index = jnp.tile(jnp.arange(max_pages, dtype=jnp.int32), packed_prompt_length.shape[0])
    page_rows = jnp.clip(lens_rep - PAGE * page_index, 0, PAGE)
    page_first = starts_rep + PAGE * page_index
    my_slots = col_index * SLOTS_DEV + jnp.arange(SLOTS_DEV, dtype=jnp.int32)
    slot_hit = prompt_page_slots.reshape(-1)[None, :] == my_slots[:, None]
    rows_used = jnp.sum(jnp.where(slot_hit, page_rows[None, :], 0), axis=1)
    first_used = jnp.sum(jnp.where(slot_hit, page_first[None, :], 0), axis=1)
    offset = jnp.clip(first_used - (col_index - 1) * tok_blk, 0, 2 * tok_blk)
    page_lines = jnp.arange(PAGE, dtype=jnp.int32)
    pick_rows = (offset[:, None] + page_lines[None, :]).reshape(-1)
    taken_rows = jnp.take(page_window, pick_rows, axis=0).reshape(
        SLOTS_DEV, PAGE, 2, head_column_span
    )
    live_rows = (page_lines[None, :] < rows_used[:, None])[:, :, None, None]
    kv_pages = jnp.where(live_rows, taken_rows, jnp.zeros_like(taken_rows))
    return (attended, kv_pages)


def solution(mesh):
    placed = (
        P(None, "col"),
        P("col", None, "row"),
        P(None, "col", None),
        P(None, None, None, "row"),
        P(),
        P(),
        P(),
        P(),
    )
    return jax.shard_map(
        local,
        mesh=mesh,
        in_specs=placed,
        out_specs=(P("col", "row"), P("col", None, None, "row")),
        check_vma=False,
    )
```

profile of v0, /device:TPU:6, one launch (start us, length us, event | category | flops | bytes accessed | tf_op | source)
XLA Modules:
  0.0 544.9 jit_solution(5829252045479823222)
XLA Ops:
  11.3 2.4 reshape.319
  13.7 7.4 %all-to-all-start.1 = ((bf16[16,2,7168]{2,1,0:T(2,128)(2,1)}), bf16[16,2,7168]{2,1,0:T(2,128)(2,1)S(1)}, u32[]{:S(2)}, u32[]{:S(2)}) async-start(bf16[16,2,7168]{2,1,0:T(2,128)(2,1)} %reshape.319), calls=%async_computation.1 | async-start | bytes 917504 | tf_op jit(solution)/shard_map/all_to_all | solution.py:77
  21.1 8.1 %copy.104 = bf16[56,16,8,512]{3,2,0,1:T(8,128)(2,1)} copy(bf16[56,16,8,512]{3,2,1,0:T(8,128)(2,1)} %bitcast.61) | data formatting | bytes 14680064 | tf_op jit(solution)/shard_map/all_to_all | solution.py:81
  31.0 5.9 %all-to-all-start = ((bf16[16,512,448]{1,2,0:T(8,128)(2,1)}), bf16[16,512,448]{1,2,0:T(8,128)(2,1)}, u32[]{:S(2)}, u32[]{:S(2)}) async-start(bf16[16,512,448]{1,2,0:T(8,128)(2,1)} %bitcast.59), calls=%async_computation | async-start | bytes 14680064 | tf_op jit(solution)/shard_map/all_to_all | solution.py:81
  38.1 4.2 reshape.320
  42.4 7.0 %copy.84 = bf16[7168,1,32]{0,2,1:T(8,128)(2,1)S(1)} copy(bf16[7168,1,32]{2,1,0:T(2,128)(2,1)} %reshape.320) | data formatting | bytes 917504 | tf_op jit(solution)/shard_map/all_to_all | solution.py:77
  50.0 1.9 select_reduce_fusion.1
  52.0 199.3 %all-reduce.1 = bf16[1024,32]{0,1:T(8,128)(2,1)S(1)} all-reduce(f32[1024,32]{0,1:T(8,128)S(1)} %select_reduce_fusion.1), channel_id=1, replica_groups=mesh['row'=8,'col'=16] {'col'}, use_global_device_ids=true, to_apply=%region_7.8 | all-reduce | flops 32768 | bytes 196608 | tf_op jit(solution)/shard_map/psum | solution.py:90
  251.3 13.7 %all_gather.7 = bf16[8192,32]{0,1:T(8,128)(2,1)S(1)} all-gather(bf16[1024,32]{0,1:T(8,128)(2,1)S(1)} %all-reduce.1), channel_id=1, replica_groups=mesh['row'=8,'col'=16] {'row'}, dimensions={0}, use_global_device_ids=true | all-gather | bytes 589824 | tf_op jit(solution)/shard_map/all_gather | solution.py:91
  265.0 66.0 %all-gather.2.cloned.1.call-done = bf16[7168,3,896]{2,0,1:T(8,128)(2,1)} async-done(((bf16[448,3,896]{2,0,1:T(8,128)(2,1)}), bf16[7168,3,896]{2,0,1:T(8,128)(2,1)}) %all-gather.2.cloned.1.call-update) | async-done | bytes 38535184 | tf_op jit(solution)/shard_map/all_gather | solution.py:82
  331.0 51.4 %copy.81 = bf16[7168,3,896]{0,2,1:T(8,128)(2,1)} copy(bf16[7168,3,896]{2,0,1:T(8,128)(2,1)} %all-gather.2.cloned.1.call-done) | data formatting | bytes 77070336 | tf_op jit(solution)/shard_map/all_gather | solution.py:82
  382.4 28.4 %fusion.38 = f32[512,2688]{1,0:T(8,128)} fusion(bf16[512,7168]{0,1:T(8,128)(2,1)} %bitcast.1, bf16[7168,2688]{0,1:T(8,128)(2,1)} %bitcast.58), kind=kOutput, calls=%fused_computation.78 | convolution fusion | flops 19730006016 | bytes 51380224 | tf_op jit(solution)/shard_map/dot_general | solution.py:84
  412.4 2.0 fusion.15
  419.9 2.0 fusion.10
  423.4 41.3 %collective-permute-done = bf16[512,2,896]{2,0,1:T(8,128)(2,1)} collective-permute-done((bf16[512,2,896]{2,0,1:T(8,128)(2,1)}, bf16[512,2,896]{2,0,1:T(8,128)(2,1)}, u32[]{:S(2)}, u32[]{:S(2)}) %collective-permute-start) | collective-permute-done | bytes 1835040 | tf_op jit(solution)/shard_map/ppermute | solution.py:17
  466.5 2.1 fusion.35
  468.6 3.8 copy.88
  472.5 3.1 maximum_maximum_fusion
  475.7 15.3 %copy.92 = bf16[1152,2,896]{2,1,0:T(2,128)(2,1)} copy(bf16[1152,2,896]{2,0,1:T(8,128)(2,1)S(1)} %maximum_maximum_fusion) | data formatting | bytes 8257536 | tf_op jit(solution)/shard_map/concatenate | solution.py:145
  490.9 2.4 copy.86
  493.3 12.7 %fusion.37 = (f32[7,512]{1,0:T(8,128)S(1)}, bf16[7,512,1024]{2,1,0:T(8,128)(2,1)}) fusion(pred[512,1024]{1,0:T(8,128)(4,1)S(1)} %copy-done.4, bf16[512,7,128]{0,2,1:T(8,128)(2,1)S(1)} %bitcast.68, bf16[1024,7,128]{0,2,1:T(8,128)(2,1)} %bitcast.62), kind=kOutput, calls=%fused_computation.77 | convolution fusion | flops 1904739328 | bytes 10631168 | tf_op jit(solution)/shard_map/sub | solution.py:134
  506.0 5.7 %fusion.12 = bf16[512,7,128]{0,2,1:T(8,128)(2,1)S(1)} fusion(bf16[1024,7,128]{0,2,1:T(8,128)(2,1)S(1)} %bitcast.63, bf16[7,512,1024]{2,1,0:T(8,128)(2,1)} %get-tuple-element.29, f32[512,7]{0,1:T(8,128)S(1)} %bitcast.72), kind=kOutput, calls=%fused_computation.25 | convolution fusion | flops 940441600 | bytes 10106880 | tf_op jit(solution)/shard_map/hqk,khd->qhd/dot_general | solution.py:136
  513.0 16.6 %gather_fusion = bf16[1280,2,896]{2,1,0:T(2,128)(2,1)} fusion(bf16[1152,2,896]{2,1,0:T(2,128)(2,1)} %copy.92, s32[2048]{0:T(1024)S(1)} %pad_clamp_fusion), kind=kCustom, calls=%fused_computation | custom fusion | bytes 9180160 | tf_op jit(solution)/shard_map/jit(_take)/gather | solution.py:161
  529.6 8.5 %broadcast_select_fusion.1 = bf16[10,128,2,896]{3,2,1,0:T(2,128)(2,1)} fusion(pred[10,128]{1,0:T(8,128)(4,1)S(1)} %iota_compare_fusion.4, bf16[10,128,2,896]{3,2,1,0:T(2,128)(2,1)} %bitcast.60, pred[10,128]{1,0:T(8,128)(4,1)S(1)} %fusion.28), kind=kLoop, calls=%fused_computation.7 | loop fusion | flops 4587520 | bytes 9177600 | tf_op jit(solution)/shard_map/jit(_where)/select_n | solution.py:165
  (68 shorter events, 19.3 us)
Async XLA Ops:
  7.2 323.8 %all-gather.2.cloned.1.call-start = ((), (), s32[]{:S(2)}) async-start(), calls=%async_computation.2 | async-start | bytes 40943616 | tf_op jit(solution)/shard_map/all_gather | solution.py:82
  13.7 17.3 %all-to-all-start.1 = ((bf16[16,2,7168]{2,1,0:T(2,128)(2,1)}), bf16[16,2,7168]{2,1,0:T(2,128)(2,1)S(1)}, u32[]{:S(2)}, u32[]{:S(2)}) async-start(bf16[16,2,7168]{2,1,0:T(2,128)(2,1)} %reshape.319), calls=%async_computation.1 | async-start | bytes 917504 | tf_op jit(solution)/shard_map/all_to_all | solution.py:77
  31.0 5.9 %copy-start.5 = (s32[64]{0:T(128)S(1)}, s32[64]{0:T(128)}, u32[]{:S(2)}) copy-start(s32[64]{0:T(128)} %param.12) | copy-start | bytes 772
  31.0 6.3 %copy-start.7 = (s32[64]{0:T(128)S(1)}, s32[64]{0:T(128)}, u32[]{:S(2)}) copy-start(s32[64]{0:T(128)} %param.13) | copy-start | bytes 772
  31.0 6.3 %copy-start.8 = (s32[16]{0:T(128)S(1)}, s32[16]{0:T(128)}, u32[]{:S(2)}) copy-start(s32[16]{0:T(128)} %param.14) | copy-start | bytes 196
  31.0 7.1 %copy-start.2 = (bf16[16,2,16,896]{3,2,1,0:T(8,128)(2,1)S(1)}, bf16[16,2,16,896]{3,2,1,0:T(8,128)(2,1)}, u32[]{:S(2)}) copy-start(bf16[16,2,16,896]{3,2,1,0:T(8,128)(2,1)} %param.11) | copy-start | bytes 2752516
  31.0 351.4 %all-to-all-start = ((bf16[16,512,448]{1,2,0:T(8,128)(2,1)}), bf16[16,512,448]{1,2,0:T(8,128)(2,1)}, u32[]{:S(2)}, u32[]{:S(2)}) async-start(bf16[16,512,448]{1,2,0:T(8,128)(2,1)} %bitcast.59), calls=%async_computation | async-start | bytes 14680064 | tf_op jit(solution)/shard_map/all_to_all | solution.py:81
  410.8 6.9 %copy-start.6 = (s32[64,4]{0,1:T(4,128)S(1)}, s32[64,4]{0,1:T(4,128)}, u32[]{:S(2)}) copy-start(s32[64,4]{0,1:T(4,128)} %param.15) | copy-start | bytes 3076
  415.8 49.0 %collective-permute-start = (bf16[512,2,896]{2,0,1:T(8,128)(2,1)}, bf16[512,2,896]{2,0,1:T(8,128)(2,1)}, u32[]{:S(2)}, u32[]{:S(2)}) collective-permute-start(bf16[512,2,896]{2,0,1:T(8,128)(2,1)} %pad_maximum_fusion), channel_id=1, source_target_pairs={{0,1},{1,2},{2,3},{3,4},{4,5},{5,6},{6,7},{7,8},{8,9},{9,10},{10,1... | collective-permute-start | bytes 5505032 | tf_op jit(solution)/shard_map/ppermute | solution.py:17
  475.6 15.3 %copy-start = (bf16[1024,1,896]{2,0,1:T(8,128)(2,1)S(1)}, bf16[1024,1,896]{2,0,1:T(8,128)(2,1)}, u32[]{:S(2)}) copy-start(bf16[1024,1,896]{2,0,1:T(8,128)(2,1)} %get-tuple-element.21) | copy-start | bytes 5505028
  475.6 17.7 %copy-start.3 = (bf16[512,896]{0,1:T(8,128)(2,1)S(1)}, bf16[512,896]{0,1:T(8,128)(2,1)}, u32[]{:S(2)}) copy-start(bf16[512,896]{0,1:T(8,128)(2,1)} %copy.87) | copy-start | bytes 2752516
  475.6 17.7 %copy-start.4 = (pred[512,1024]{1,0:T(8,128)(4,1)S(1)}, pred[512,1024]{1,0:T(8,128)(4,1)}, u32[]{:S(2)}) copy-start(pred[512,1024]{1,0:T(8,128)(4,1)} %compare_and_fusion) | copy-start | bytes 1572868
  493.3 12.7 %copy-start.1 = (bf16[1024,1,896]{0,2,1:T(8,128)(2,1)S(1)}, bf16[1024,1,896]{0,2,1:T(8,128)(2,1)}, u32[]{:S(2)}) copy-start(bf16[1024,1,896]{0,2,1:T(8,128)(2,1)} %copy.86) | copy-start | bytes 5505028
Sparse Core Ops, SparseCore 0:
  10.1 320.8 all-gather.1
where the time goes:
time: 547 us; the launch traced here: 545 us
  blocking collectives  213 us (39%)
  local copies, waits for them, and re-layouts  120 us (22%)
  waiting for transfers between devices  110 us (20%)
  matrix products  52.6 us (10%)
  other arithmetic  19.5 us (4%)
  starting transfers between devices  15.3 us (3%)
  between operations  14.3 us (3%)
    psum x1, blocking collectives, local(): lax.psum(down_term(row_part, row_slots, down_cols, active_slots), 'col')  199 us
    all_gather x1, waiting for transfers between devices, local(): weight_piece = lax.all_gather(projection_weight, 'col', axis=0, tiled=True)  66 us
    all_gather x1, local copies, waits for them, and re-layouts, local(): weight_piece = lax.all_gather(projection_weight, 'col', axis=0, tiled=True)  51.4 us
    ppermute x1, waiting for transfers between devices, shifted(): return lax.ppermute(block, axis, route)  41.3 us
    dot_general x1, matrix products, local(): jnp.dot(own_rows, flat_piece, preferred_element_type=jnp.float32)  28.4 us
    gather x1, local copies, waits for them, and re-layouts, local(): jnp.take(page_window, pick_rows, axis=0)  16.6 us
    concatenate x2, local copies, waits for them, and re-layouts, local(): jnp.concatenate([prev_kv, own_kv, jnp.zeros((PAGE, 2, head_column_span),...  15.3 us
    all_gather x1, blocking collectives, local(): lax.all_gather(summed.astype(jnp.bfloat16), 'row', axis=0, tiled=True)  13.7 us
  transfers between devices with their start and end apart: 4, of which 3 were waited for; matrix products, arithmetic and copies ran while one was open for 16% of the time, Pallas kernels for 0%

commit v1 on v0

--- a/solution.py
+++ b/solution.py
@@ -79,7 +79,9 @@
     )
     down_cols = down_weight_slices.reshape(width_loc, -1)
     own_rows = lax.all_to_all(normed, "col", split_axis=0, concat_axis=1, tiled=True)
-    weight_piece = lax.all_gather(projection_weight, "col", axis=0, tiled=True)
+    weight_piece = jnp.concatenate(
+        lax.all_to_all(jnp.stack([projection_weight] * lax.axis_size("col")), "col", 0, 0), axis=0
+    )
     flat_piece = weight_piece.reshape(weight_piece.shape[0], -1)
     projection_total = jnp.dot(own_rows, flat_piece, preferred_element_type=jnp.float32)
     rows_per = tok_all // row_count

time: 547 us -> 1220 us (2.23)
  waiting for transfers between devices: 110 us -> 734 us
  local copies, waits for them, and re-layouts: 120 us -> 210 us
  blocking collectives: 213 us -> 169 us
  between operations: 14.3 us -> 0.91 us
  starting transfers between devices: 15.3 us -> 28.3 us
    all_to_all x1, waiting for transfers between devices: 1.74 us -> 695 us  [local(): lax.all_to_all(jnp.stack([projection_weight] * lax.axis_size('col')), 'co...]
    another operation x1 -> x3, local copies, waits for them, and re-layouts: 0.1 us -> 83.9 us  [the longest x1 69.9 us: local(): flat_piece = weight_piece.reshape(weight_piece.shape[0], -1)]
    all_gather x1 -> x0, waiting for transfers between devices: 66 us -> none  [local(): weight_piece = lax.all_gather(projection_weight, 'col', axis=0, tiled=True)]
    psum x1, blocking collectives: 199 us -> 138 us  [local(): lax.psum(down_term(row_part, row_slots, down_cols, active_slots), 'col')]
    all_to_all x0 -> x1, local copies, waits for them, and re-layouts: none -> 59.7 us  [local(): lax.all_to_all(jnp.stack([projection_weight] * lax.axis_size('col')), 'co...]
    all_gather x1 -> x0, local copies, waits for them, and re-layouts: 51.4 us -> none  [local(): weight_piece = lax.all_gather(projection_weight, 'col', axis=0, tiled=True)]
    all_to_all x0 -> x1, blocking collectives: none -> 16 us  [local(): lax.all_to_all(adapter_down_weight, 'col', split_axis=0, concat_axis=1, t...]
    all_to_all x1, starting transfers between devices: 5.93 us -> 18.4 us  [local(): lax.all_to_all(normed, 'col', split_axis=0, concat_axis=1, tiled=True)]
  transfers between devices with their start and end apart: 4 -> 3, of which waited for: 3 -> 2; matrix products, arithmetic and copies ran while one was open for 16% -> 13% of each run, Pallas kernels for 0% -> 0%
where the time goes in v1:
time: 1220 us; the launch traced here: 1210 us
  waiting for transfers between devices  734 us (60%)
  local copies, waits for them, and re-layouts  210 us (17%)
  blocking collectives  169 us (14%)
  matrix products  52.6 us (4%)
  starting transfers between devices  28.3 us (2%)
  other arithmetic  19.5 us (2%)
    all_to_all x1, waiting for transfers between devices, local(): lax.all_to_all(jnp.stack([projection_weight] * lax.axis_size('col')), 'co...  695 us
    psum x1, blocking collectives, local(): lax.psum(down_term(row_part, row_slots, down_cols, active_slots), 'col')  138 us
    another operation x1, local copies, waits for them, and re-layouts, local(): flat_piece = weight_piece.reshape(weight_piece.shape[0], -1)  69.9 us
    all_to_all x1, local copies, waits for them, and re-layouts, local(): lax.all_to_all(jnp.stack([projection_weight] * lax.axis_size('col')), 'co...  59.7 us
    ppermute x1, waiting for transfers between devices, shifted(): return lax.ppermute(block, axis, route)  38.9 us
    dot_general x1, matrix products, local(): jnp.dot(own_rows, flat_piece, preferred_element_type=jnp.float32)  28.4 us
  transfers between devices with their start and end apart: 3, of which 2 were waited for; matrix products, arithmetic and copies ran while one was open for 13% of the time, Pallas kernels for 0%

profile of v1, /device:TPU:6, one launch (start us, length us, event | category | flops | bytes accessed | tf_op | source)
XLA Modules:
  0.0 1214.2 jit_solution(4682268852704500293)
XLA Ops:
  5.8 16.0 %all_to_all.39 = bf16[16,2,7168]{2,1,0:T(2,128)(2,1)S(1)} all-to-all(bf16[16,2,7168]{2,1,0:T(2,128)(2,1)S(1)} %reshape.317), channel_id=1, replica_groups=mesh['row'=8,'col'=16] {'col'}, dimensions={0} | all-to-all | bytes 917504 | tf_op jit(solution)/shard_map/all_to_all | solution.py:77
  21.8 13.8 %stack.8 = bf16[16,448,3,896]{3,1,2,0:T(8,128)(2,1)} broadcast(bf16[448,3,896]{2,0,1:T(8,128)(2,1)} %param.9), dimensions={1,2,3} | broadcast | bytes 40943616 | tf_op jit(solution)/shard_map/stack | solution.py:83
  35.6 8.0 all-to-all-start.1
  43.6 6.9 copy.105
  50.5 695.3 %all-to-all-done.1 = bf16[16,448,3,896]{3,1,2,0:T(8,128)(2,1)} async-done(((bf16[16,448,3,896]{3,1,2,0:T(8,128)(2,1)}), bf16[16,448,3,896]{3,1,2,0:T(8,128)(2,1)}, u32[]{:S(2)}, u32[]{:S(2)}) %all-to-all-start.1) | async-done | bytes 38535200 | tf_op jit(solution)/shard_map/all_to_all | solution.py:83
  745.8 18.4 %all-to-all-start = ((bf16[16,512,448]{1,2,0:T(8,128)(2,1)}), bf16[16,512,448]{1,2,0:T(8,128)(2,1)}, u32[]{:S(2)}, u32[]{:S(2)}) async-start(bf16[16,512,448]{1,2,0:T(8,128)(2,1)} %bitcast.61), calls=%async_computation | async-start | bytes 14680064 | tf_op jit(solution)/shard_map/all_to_all | solution.py:81
  765.4 4.2 reshape.318
  769.6 7.0 copy.85
  779.2 138.0 %all-reduce.1 = bf16[1024,32]{0,1:T(8,128)(2,1)S(1)} all-reduce(f32[1024,32]{0,1:T(8,128)S(1)} %select_reduce_fusion.1), channel_id=1, replica_groups=mesh['row'=8,'col'=16] {'col'}, use_global_device_ids=true, to_apply=%region_7.8 | all-reduce | flops 32768 | bytes 196608 | tf_op jit(solution)/shard_map/psum | solution.py:92
  917.2 14.5 %all_gather.3 = bf16[8192,32]{0,1:T(8,128)(2,1)S(1)} all-gather(bf16[1024,32]{0,1:T(8,128)(2,1)S(1)} %all-reduce.1), channel_id=1, replica_groups=mesh['row'=8,'col'=16] {'row'}, dimensions={0}, use_global_device_ids=true | all-gather | bytes 589824 | tf_op jit(solution)/shard_map/all_gather | solution.py:93
  931.8 59.7 %copy.82 = bf16[16,448,3,896]{1,0,3,2:T(8,128)(2,1)} copy(bf16[16,448,3,896]{3,1,2,0:T(8,128)(2,1)} %all-to-all-done.1) | data formatting | bytes 77070336 | tf_op jit(solution)/shard_map/all_to_all | solution.py:83
  991.5 69.9 %reshape_reshape.3 = bf16[7168,2688]{0,1:T(8,128)(2,1)} reshape(bf16[16,448,3,896]{1,0,3,2:T(8,128)(2,1)} %copy.82) | data formatting | bytes 77070336 | tf_op jit(solution)/shard_map/reshape;reshape | solution.py:85
  1061.4 28.4 %fusion.38 = f32[512,2688]{1,0:T(8,128)} fusion(bf16[512,7168]{0,1:T(8,128)(2,1)} %bitcast.1, bf16[7168,2688]{0,1:T(8,128)(2,1)} %reshape_reshape.3), kind=kOutput, calls=%fused_computation.78 | convolution fusion | flops 19730006016 | bytes 51380224 | tf_op jit(solution)/shard_map/dot_general | solution.py:86
  1091.4 2.0 fusion.15
  1099.0 2.0 fusion.10
  1102.5 38.9 %collective-permute-done = bf16[512,2,896]{2,0,1:T(8,128)(2,1)} collective-permute-done((bf16[512,2,896]{2,0,1:T(8,128)(2,1)}, bf16[512,2,896]{2,0,1:T(8,128)(2,1)}, u32[]{:S(2)}, u32[]{:S(2)}) %collective-permute-start) | collective-permute-done | bytes 1835040 | tf_op jit(solution)/shard_map/ppermute | solution.py:17
  1141.4 3.1 maximum_maximum_fusion
  1144.6 15.3 %copy.93 = bf16[1152,2,896]{2,1,0:T(2,128)(2,1)} copy(bf16[1152,2,896]{2,0,1:T(8,128)(2,1)S(1)} %maximum_maximum_fusion) | data formatting | bytes 8257536 | tf_op jit(solution)/shard_map/concatenate | solution.py:147
  1163.2 3.9 copy.89
  1167.1 2.4 copy.87
  1169.5 12.7 %fusion.37 = (f32[7,512]{1,0:T(8,128)S(1)}, bf16[7,512,1024]{2,1,0:T(8,128)(2,1)}) fusion(pred[512,1024]{1,0:T(8,128)(4,1)S(1)} %copy-done.3, bf16[512,7,128]{0,2,1:T(8,128)(2,1)S(1)} %bitcast.70, bf16[1024,7,128]{0,2,1:T(8,128)(2,1)} %bitcast.64), kind=kOutput, calls=%fused_computation.77 | convolution fusion | flops 1904739328 | bytes 10631168 | tf_op jit(solution)/shard_map/sub | solution.py:136
  1182.2 5.7 fusion.12
  1189.1 16.6 %gather_fusion = bf16[1280,2,896]{2,1,0:T(2,128)(2,1)} fusion(bf16[1152,2,896]{2,1,0:T(2,128)(2,1)} %copy.93, s32[2048]{0:T(1024)S(1)} %pad_clamp_fusion), kind=kCustom, calls=%fused_computation | custom fusion | bytes 9180160 | tf_op jit(solution)/shard_map/jit(_take)/gather | solution.py:163
  1205.7 8.5 broadcast_select_fusion.1
  (66 shorter events, 22.1 us)
Async XLA Ops:
  35.6 710.2 %all-to-all-start.1 = ((bf16[16,448,3,896]{3,1,2,0:T(8,128)(2,1)}), bf16[16,448,3,896]{3,1,2,0:T(8,128)(2,1)}, u32[]{:S(2)}, u32[]{:S(2)}) async-start(bf16[16,448,3,896]{3,1,2,0:T(8,128)(2,1)} %stack.8), calls=%async_computation.1 | async-start | bytes 77070336 | tf_op jit(solution)/shard_map/all_to_all | solution.py:83
  745.8 18.4 %copy-start.4 = (s32[64]{0:T(128)S(1)}, s32[64]{0:T(128)}, u32[]{:S(2)}) copy-start(s32[64]{0:T(128)} %param.12) | copy-start | bytes 772
  745.8 18.7 %copy-start.6 = (s32[64]{0:T(128)S(1)}, s32[64]{0:T(128)}, u32[]{:S(2)}) copy-start(s32[64]{0:T(128)} %param.13) | copy-start | bytes 772
  745.8 18.7 %copy-start.7 = (s32[16]{0:T(128)S(1)}, s32[16]{0:T(128)}, u32[]{:S(2)}) copy-start(s32[16]{0:T(128)} %param.14) | copy-start | bytes 196
  745.8 19.5 %copy-start.1 = (bf16[16,2,16,896]{3,2,1,0:T(8,128)(2,1)S(1)}, bf16[16,2,16,896]{3,2,1,0:T(8,128)(2,1)}, u32[]{:S(2)}) copy-start(bf16[16,2,16,896]{3,2,1,0:T(8,128)(2,1)} %param.11) | copy-start | bytes 2752516
  745.8 315.6 %all-to-all-start = ((bf16[16,512,448]{1,2,0:T(8,128)(2,1)}), bf16[16,512,448]{1,2,0:T(8,128)(2,1)}, u32[]{:S(2)}, u32[]{:S(2)}) async-start(bf16[16,512,448]{1,2,0:T(8,128)(2,1)} %bitcast.61), calls=%async_computation | async-start | bytes 14680064 | tf_op jit(solution)/shard_map/all_to_all | solution.py:81
  1089.8 7.0 copy-start.5
  1094.8 46.6 %collective-permute-start = (bf16[512,2,896]{2,0,1:T(8,128)(2,1)}, bf16[512,2,896]{2,0,1:T(8,128)(2,1)}, u32[]{:S(2)}, u32[]{:S(2)}) collective-permute-start(bf16[512,2,896]{2,0,1:T(8,128)(2,1)} %pad_maximum_fusion), channel_id=1, source_target_pairs={{0,1},{1,2},{2,3},{3,4},{4,5},{5,6},{6,7},{7,8},{8,9},{9,10},{10,1... | collective-permute-start | bytes 5505032 | tf_op jit(solution)/shard_map/ppermute | solution.py:17
  1163.2 6.3 copy-start.2
  1163.2 6.3 copy-start.3
  1169.5 12.7 %copy-start = (bf16[1024,1,896]{0,2,1:T(8,128)(2,1)S(1)}, bf16[1024,1,896]{0,2,1:T(8,128)(2,1)}, u32[]{:S(2)}) copy-start(bf16[1024,1,896]{0,2,1:T(8,128)(2,1)} %copy.87) | copy-start | bytes 5505028
